TPU v7x, 256 devices: a whole 4x4x8 slice. The times are simulated.
256 devices in a mesh: seq: 64 (over y, z, core), tensor: 4 (over x).
Axes of the slice: x: 4, y: 4, z: 8, core: 2. Of those that a mesh axis runs over, the one named last changes fastest.
Arguments:
- tokens: bfloat16 [32768, 3840], P('seq', 'tensor'), may hold values from -6 to 6
- w_query: bfloat16 [3840, 2048], P(None, 'tensor'), may hold values from -0.09375 to 0.09375
- w_key: bfloat16 [3840, 1024], P(None, 'tensor'), may hold values from -0.09375 to 0.09375
- w_value: bfloat16 [3840, 1024], P(None, 'tensor'), may hold values from -0.09375 to 0.09375
- query_gain: float32 [256], replicated, may hold values from 0.1 to 1.9
- key_gain: float32 [256], replicated, may hold values from 0.1 to 1.9
- adapter_down: bfloat16 [64, 64, 3840], P('seq', None, 'tensor'), may hold values from -0.09375 to 0.09375
- adapter_up: bfloat16 [64, 64, 2048], P('seq', None, 'tensor'), may hold values from -0.75 to 0.75
- adapter_ids: int32 [32768, 1], P('seq'), may hold values from 0 to 63; in each aligned block of 512 rows (0 to 511, 512 to 1023, ...) at most 16 rows name the same one
- doc_ids: int32 [32768], P('seq'), may hold values from 0 to 63, never falling along the last dimension, each value on 1 to 4096 neighbouring positions
- cotangent: bfloat16 [32768, 2048], P('seq', 'tensor'), may hold values from -6 to 6
Outputs:
- attended: bfloat16 [32768, 2048], P('seq', 'tensor')
- grad_up: float32 [64, 64, 2048], P('seq', None, 'tensor')
Inputs may be any that keep to these rules, and one draw needn't show every extreme that they name: `adapter_ids`: within the 512 tokens of one device no adapter is named by more than 16 tokens; in every draw some adapter is named by exactly 16 tokens of some device. `doc_ids`: document numbers never fall along the slab; each document has 1 to 4096 tokens and one has exactly 4096.
All inputs are finite; a program needn't handle non-finite values.
Results may differ from a plain program's by a relative error of at most 0.0088.
Values may be sent and summed in bfloat16 or wider, within the bound.
A program may use at most 128 MiB of HBM per device.

v0:
```python
import math
import jax
import jax.numpy as jnp
from jax import lax
from jax.sharding import PartitionSpec as P

HD = 256
R = 64
WINDOW = 1024
ADAPTERS = 64
CAP = 16


def passed_along(value, axis, steps):
    count = lax.axis_size(axis)
    first, last = (max(0, -steps), min(count, count - steps))
    return lax.ppermute(value, axis, [(source, source + steps) for source in range(first, last)])


def normalize(pre_field, gain_vec):
    mean_sq = jnp.mean(pre_field * pre_field, axis=-1, keepdims=True)
    return pre_field * lax.rsqrt(mean_sq + 1e-06) * gain_vec


def rotate(pre_field, positions):
    half_dim = pre_field.shape[-1] // 2
    frequency = jnp.exp(
        jnp.arange(half_dim, dtype=jnp.float32) * (-2.0 * math.log(10000.0) / pre_field.shape[-1])
    )
    angles = positions.astype(jnp.float32)[:, None] * frequency[None, :]
    cosine = jnp.cos(angles)[:, None, :]
    sine_part = jnp.sin(angles)[:, None, :]
    lower_half = pre_field[..., :half_dim]
    second = pre_field[..., half_dim:]
    return jnp.concatenate(
        [lower_half * cosine - second * sine_part, second * cosine + lower_half * sine_part],
        axis=-1,
    )


def shape_query(pre_field, gain_vec, positions):
    return rotate(normalize(pre_field, gain_vec), positions)


def attend(queries, key_rows, values, upstream, allowed):
    score_scale = 1.0 / math.sqrt(queries.shape[-1])
    scores = (
        jnp.einsum("tngd,knd->ngtk", queries, key_rows, preferred_element_type=jnp.float32)
        * score_scale
    )
    weights = jnp.where(allowed[None, None], jnp.exp(scores), 0.0)
    probs = weights / jnp.sum(weights, axis=-1, keepdims=True)
    probs_low = probs.astype(jnp.bfloat16)
    attended = jnp.einsum("ngtk,knd->tngd", probs_low, values, preferred_element_type=jnp.float32)
    dprobs = jnp.einsum("tngd,knd->ngtk", upstream, values, preferred_element_type=jnp.float32)
    delta = jnp.sum(probs * dprobs, axis=-1, keepdims=True)
    dscores = (probs * (dprobs - delta) * score_scale).astype(jnp.bfloat16)
    dqueries = jnp.einsum("ngtk,knd->tngd", dscores, key_rows, preferred_element_type=jnp.float32)
    return (attended.astype(jnp.bfloat16), dqueries)


def local(
    tokens,
    w_query,
    w_key,
    w_value,
    query_gain,
    key_gain,
    adapter_down,
    adapter_up,
    adapter_ids,
    doc_ids,
    cotangent,
):
    tok_count = tokens.shape[0]
    feat_width = tokens.shape[1]
    q_width = w_query.shape[1]
    kv_width = w_key.shape[1]
    local_heads = q_width // HD
    kv_heads = kv_width // HD
    head_group = local_heads // kv_heads
    positions = lax.axis_index("seq") * tok_count + jnp.arange(tok_count, dtype=jnp.int32)
    shard_cols = lax.all_gather(tokens, "tensor", axis=1, tiled=True)
    query_lin = jnp.dot(shard_cols, w_query, preferred_element_type=jnp.float32)
    key_lin = jnp.dot(shard_cols, w_key, preferred_element_type=jnp.float32)
    value_lin = jnp.dot(shard_cols, w_value, preferred_element_type=jnp.float32)
    token_adapter = adapter_ids[:, 0]
    chosen = token_adapter[:, None] == jnp.arange(ADAPTERS, dtype=jnp.int32)[None, :]
    before = jnp.cumsum(chosen.astype(jnp.int32), axis=0) - 1
    slot_rank = jnp.sum(jnp.where(chosen, before, 0), axis=1)
    slot_index = token_adapter * CAP + slot_rank
    dispatch = (slot_index[None, :] == jnp.arange(ADAPTERS * CAP, dtype=jnp.int32)[:, None]).astype(
        jnp.bfloat16
    )
    outgoing = jnp.dot(dispatch, tokens, preferred_element_type=jnp.float32).astype(jnp.bfloat16)
    all_down, all_up = (
        lax.all_gather(adapter_down, "seq", axis=0, tiled=True),
        lax.all_gather(adapter_up, "seq", axis=0, tiled=True),
    )
    slot_rows = outgoing.reshape(ADAPTERS, CAP, feat_width)
    partial_low = jnp.einsum(
        "acd,ard->acr", slot_rows, all_down, preferred_element_type=jnp.float32
    )
    slot_low = lax.psum(partial_low, "tensor").astype(jnp.bfloat16)
    slot_lift = jnp.einsum(
        "acr,are->ace", slot_low, all_up, preferred_element_type=jnp.float32
    ).astype(jnp.bfloat16)
    lifted = jnp.einsum(
        "st,se->te",
        dispatch,
        slot_lift.reshape(ADAPTERS * CAP, q_width),
        preferred_element_type=jnp.float32,
    ).astype(jnp.bfloat16)
    lowrank = jnp.einsum(
        "st,sr->tr",
        dispatch,
        slot_low.reshape(ADAPTERS * CAP, R),
        preferred_element_type=jnp.float32,
    ).astype(jnp.bfloat16)
    query_pre = (query_lin + lifted.astype(jnp.float32)).reshape(tok_count, local_heads, HD)
    queries, query_back = jax.vjp(
        lambda pre_query: shape_query(pre_query, query_gain, positions), query_pre
    )
    queries = queries.astype(jnp.bfloat16).reshape(tok_count, kv_heads, head_group, HD)
    key_rows = shape_query(key_lin.reshape(tok_count, kv_heads, HD), key_gain, positions).astype(
        jnp.bfloat16
    )
    values = value_lin.astype(jnp.bfloat16).reshape(tok_count, kv_heads, HD)
    rim_count = WINDOW // tok_count
    key_list = []
    value_list = []
    doc_list = []
    place_list = []
    for distance in range(rim_count, 0, -1):
        far_keys, far_values, far_docs = passed_along((key_rows, values, doc_ids), "seq", distance)
        key_list.append(far_keys)
        value_list.append(far_values)
        doc_list.append(far_docs)
        place_list.append(positions - distance * tok_count)
    key_list.append(key_rows)
    value_list.append(values)
    doc_list.append(doc_ids)
    place_list.append(positions)
    window_keys = jnp.concatenate(key_list, axis=0)
    window_values = jnp.concatenate(value_list, axis=0)
    key_docs = jnp.concatenate(doc_list, axis=0)
    key_pos = jnp.concatenate(place_list, axis=0)
    key_gap = positions[:, None] - key_pos[None, :]
    allowed = (
        (doc_ids[:, None] == key_docs[None, :])
        & (key_gap >= 0)
        & (key_gap < WINDOW)
        & (key_pos[None, :] >= 0)
    )
    upstream = cotangent.reshape(tok_count, kv_heads, head_group, HD)
    block_out, dqueries = attend(queries, window_keys, window_values, upstream, allowed)
    attended = block_out.reshape(tok_count, q_width)
    (dquery_pre,) = query_back(dqueries.reshape(tok_count, local_heads, HD))
    dquery_pre = dquery_pre.reshape(tok_count, q_width).astype(jnp.bfloat16)
    out_low = jnp.dot(dispatch, lowrank, preferred_element_type=jnp.float32).astype(jnp.bfloat16)
    out_grad = jnp.dot(dispatch, dquery_pre, preferred_element_type=jnp.float32).astype(
        jnp.bfloat16
    )
    slot_low_rows = out_low.reshape(ADAPTERS, CAP, R)
    slot_grad_rows = out_grad.reshape(ADAPTERS, CAP, q_width)
    grad_up = lax.psum_scatter(
        jnp.einsum(
            "acr,ace->are", slot_low_rows, slot_grad_rows, preferred_element_type=jnp.float32
        ),
        "seq",
        scatter_dimension=0,
        tiled=True,
    )
    return (attended, grad_up)


def solution(mesh):
    in_specs = (
        P("seq", "tensor"),
        P(None, "tensor"),
        P(None, "tensor"),
        P(None, "tensor"),
        P(),
        P(),
        P("seq", None, "tensor"),
        P("seq", None, "tensor"),
        P("seq", None),
        P("seq"),
        P("seq", "tensor"),
    )
    out_specs = (P("seq", "tensor"), P("seq", None, "tensor"))
    return jax.shard_map(local, mesh=mesh, in_specs=in_specs, out_specs=out_specs, check_vma=False)
```

profile of v0, /device:TPU:2, one launch (start us, length us, event | category | flops | bytes accessed | tf_op | source)
XLA Modules:
  0.0 409.1 jit_solution(11032409171625994337)
XLA Ops:
  7.2 0.0 copy-start
  7.2 0.0 all-gather.4.cloned.1.call-start
  7.2 0.7 all-gather.4.cloned.1.call-update
  7.9 0.0 all-gather.6.cloned.1.call-start
  8.0 0.7 all-gather.6.cloned.1.call-update
  8.7 0.0 all-gather.8.cloned.1.call-start
  8.7 0.7 all-gather.8.cloned.1.call-update
  9.4 0.0 reduce-scatter.2.cloned.1.call-start
  9.4 1.7 collective-permute-start.3
  11.2 4.0 collective-permute-start.2
  15.2 0.7 fusion.60
  15.9 1.2 reduce-window.6
  17.1 0.2 slice_reduce_fusion
  17.4 0.8 fusion.59
  18.2 0.7 multiply_add_fusion.3
  18.9 1.0 multiply_cosine_fusion
  19.9 3.7 fusion.24
  23.7 4.0 copy.40
  27.7 0.0 collective-permute-done.3
  27.7 0.0 collective-permute-done.2
  27.7 2.5 fusion.16
  30.2 30.4 %all-gather.4.cloned.1.call-done = bf16[512,3840]{0,1:T(8,128)(2,1)} async-done(((bf16[512,960]{0,1:T(8,128)(2,1)}), bf16[512,3840]{0,1:T(8,128)(2,1)}) %all-gather.4.cloned.1.call-update) | async-done | bytes 3932176 | tf_op jit(solution)/shard_map/all_gather | solution.py:83
  60.7 3.5 multiply_reduce_fusion.2
  64.2 0.1 multiply_bitcast_fusion
  64.3 1.2 fusion.55
  65.5 0.7 pad_maximum_fusion
  66.2 2.3 collective-permute-start.5
  68.5 3.8 collective-permute-start.4
  72.3 1.9 fusion.34
  74.2 4.0 collective-permute-start.1
  78.2 2.8 collective-permute-start
  81.0 66.8 %all-gather.6.cloned.1.call-done = bf16[64,64,960]{2,1,0:T(8,128)(2,1)} async-done(((bf16[1,64,960]{2,1,0:T(8,128)(2,1)}), bf16[64,64,960]{2,1,0:T(8,128)(2,1)}) %all-gather.6.cloned.1.call-update) | async-done | bytes 7864336 | tf_op jit(solution)/shard_map/all_gather | solution.py:97
  147.8 6.3 %fusion.73 = f32[64,16,64]{2,1,0:T(8,128)S(1)} fusion(bf16[64,16,960]{2,1,0:T(8,128)(2,1)} %bitcast.128, bf16[64,64,960]{2,1,0:T(8,128)(2,1)} %all-gather.6.cloned.1.call-done), kind=kOutput, calls=%fused_computation.106 | convolution fusion | flops 125829120 | bytes 10092544 | tf_op jit(solution)/shard_map/acd,ard->acr/dot_general | solution.py:101
  154.1 20.2 %all-reduce.3 = bf16[64,16,64]{2,1,0:T(8,128)(2,1)S(1)} all-reduce(f32[64,16,64]{2,1,0:T(8,128)S(1)} %fusion.73), channel_id=1, replica_groups=mesh['seq'=64,'tensor'=4] {'tensor'}, use_global_device_ids=true, to_apply=%region_4.5 | all-reduce | flops 65536 | bytes 393216 | tf_op jit(solution)/shard_map/psum | solution.py:104
  174.4 52.3 %all-gather.8.cloned.1.call-done = bf16[64,64,512]{2,1,0:T(8,128)(2,1)} async-done(((bf16[1,64,512]{2,1,0:T(8,128)(2,1)}), bf16[64,64,512]{2,1,0:T(8,128)(2,1)}) %all-gather.8.cloned.1.call-update) | async-done | bytes 4194320 | tf_op jit(solution)/shard_map/all_gather | solution.py:98
  226.7 3.0 convolution_convert_fusion
  229.7 0.8 fusion.30
  230.5 0.8 copy-done.8
  231.2 2.3 multiply_reduce_fusion.1
  233.5 0.0 copy-start.3
  233.5 0.3 copy.41
  233.9 0.9 fusion.35
  234.8 0.2 copy.45
  234.9 0.2 multiply_multiply_fusion
  235.2 0.1 subtract_convert_fusion
  235.3 0.0 collective-permute-done.5
  235.3 0.0 collective-permute-done.4
  235.3 0.0 copy-start.10
  235.3 3.1 fusion.5
  238.4 0.0 collective-permute-done.1
  238.5 0.0 collective-permute-done
  238.5 4.4 %fusion = (f32[2,512]{1,0:T(2,128)S(1)}, f32[1536,512,2]{1,0,2:T(8,128)S(1)}) fusion(f32[2,512]{1,0:T(2,128)S(1)} %get-tuple-element.20, f32[1536,512,2]{1,0,2:T(8,128)S(1)} %get-tuple-element.21, pred[512,1536]{0,1:T(8,128)(4,1)S(1)} %copy-done.2, bf16[64,2,8,256]{3,2,1,0:T(8,128)(2,1)S(1)} %bitcast.139, bf16[512,1,256]{2,0,1:T(8,128)(2,1)} %fusion.34, ...), kind=kOutput, calls=%fused_computation.3 | convolution fusion | flops 815528960 | bytes 14688256 | tf_op jit(solution)/shard_map/tngd,knd->ngtk/dot_general | solution.py:55
  242.9 3.8 fusion.26
  246.7 0.2 multiply_add_fusion.1
  246.8 0.3 multiply_reduce_fusion
  247.1 0.4 fusion.37
  247.5 0.2 copy.51
  247.7 0.7 fusion.25
  248.4 4.5 %fusion.74 = f32[64,64,512]{2,1,0:T(8,128)} fusion(bf16[64,16,64]{2,1,0:T(8,128)(2,1)S(1)} %bitcast.130, bf16[64,16,512]{2,1,0:T(8,128)(2,1)S(1)} %bitcast.129), kind=kOutput, calls=%fused_computation.107 | convolution fusion | flops 67108864 | bytes 9568256 | tf_op jit(solution)/shard_map/acr,ace->are/dot_general | solution.py:167
  253.0 0.0 reduce-scatter.2.cloned.1.call-update
  253.0 0.0 copy-start.1
  253.0 5.2 %fusion.31 = bf16[256,2,512]{2,0,1:T(8,128)(2,1)S(1)} fusion(f32[2,512]{1,0:T(2,128)S(1)} %get-tuple-element.20, f32[1536,512,2]{1,0,2:T(8,128)} %copy-done.11, pred[512,1536]{0,1:T(8,128)(4,1)S(1)} %copy-done.2, bf16[512,1,256]{2,0,1:T(8,128)(2,1)} %fusion.34, bf16[512,1,256]{2,0,1:T(8,128)(2,1)} %collective-permute-done.1, ...), kind=kOutput, calls=%fused_computation.35 | convolution fusion | flops 814219264 | bytes 8392704 | tf_op jit(solution)/shard_map/ngtk,knd->tngd/dot_general | solution.py:54
  258.2 1.0 copy.52
  259.2 143.4 %reduce-scatter.2.cloned.1.call-done = f32[1,64,512]{2,1,0:T(8,128)} async-done(((f32[64,64,512]{2,1,0:T(8,128)}), f32[1,64,512]{2,1,0:T(8,128)}) %reduce-scatter.2.cloned.1.call-update) | async-done | bytes 131088 | tf_op jit(solution)/shard_map/reduce_scatter | solution.py:166
  (31 shorter events, 0.2 us)
Async XLA Ops:
  7.2 53.5 %copy-start = (bf16[3840,256]{1,0:T(8,128)(2,1)S(1)}, bf16[3840,256]{1,0:T(8,128)(2,1)}, u32[]{:S(2)}) copy-start(bf16[3840,256]{1,0:T(8,128)(2,1)} %param.13) | copy-start | bytes 5898244
  7.2 53.5 %all-gather.4.cloned.1.call-start = ((), (), s32[]{:S(2)}) async-start(), calls=%async_computation.1 | async-start | bytes 4915200 | tf_op jit(solution)/shard_map/all_gather | solution.py:83
  7.9 139.9 %all-gather.6.cloned.1.call-start = ((), (), s32[]{:S(2)}) async-start(), calls=%async_computation.2 | async-start | bytes 8519680 | tf_op jit(solution)/shard_map/all_gather | solution.py:97
  8.7 218.0 %all-gather.8.cloned.1.call-start = ((), (), s32[]{:S(2)}) async-start(), calls=%async_computation.3 | async-start | bytes 4259840 | tf_op jit(solution)/shard_map/all_gather | solution.py:98
  9.4 393.2 %reduce-scatter.2.cloned.1.call-start = ((), (), s32[]{:S(2)}) async-start(), calls=%async_computation.4 | async-start | bytes 8519680 | tf_op jit(solution)/shard_map/reduce_scatter | solution.py:166
  9.4 18.2 %collective-permute-start.3 = (s32[512]{0:T(512)}, s32[512]{0:T(512)S(1)}, u32[]{:S(2)}, u32[]{:S(2)}) collective-permute-start(s32[512]{0:T(512)} %param.20), channel_id=1, source_target_pairs={{0,4},{4,8},{8,12},{12,16},{16,20},{20,24},{24,28},{28,32},{32,36}... | collective-permute-start | bytes 6152 | tf_op jit(solution)/shard_map/ppermute | solution.py:17
  11.2 16.5 %collective-permute-start.2 = (s32[512]{0:T(512)}, s32[512]{0:T(512)S(1)}, u32[]{:S(2)}, u32[]{:S(2)}) collective-permute-start(s32[512]{0:T(512)} %param.20), channel_id=1, source_target_pairs={{0,8},{4,12},{8,16},{12,20},{16,24},{20,28},{24,32},{28,36},{32,40... | collective-permute-start | bytes 6152 | tf_op jit(solution)/shard_map/ppermute | solution.py:17
  23.7 4.0 copy-start.4
  30.2 34.0 %copy-start.5 = (f32[256]{0:T(256)S(1)}, f32[256]{0:T(256)}, u32[]{:S(2)}) copy-start(f32[256]{0:T(256)} %param.16) | copy-start | bytes 3076
  60.7 11.6 %copy-start.7 = (bf16[512,3840]{0,1:T(8,128)(2,1)S(1)}, bf16[512,3840]{0,1:T(8,128)(2,1)}, u32[]{:S(2)}) copy-start(bf16[512,3840]{0,1:T(8,128)(2,1)} %all-gather.4.cloned.1.call-done) | copy-start | bytes 11796484
  60.7 11.6 %copy-start.9 = (bf16[3840,256]{1,0:T(8,128)(2,1)S(1)}, bf16[3840,256]{1,0:T(8,128)(2,1)}, u32[]{:S(2)}) copy-start(bf16[3840,256]{1,0:T(8,128)(2,1)} %param.14) | copy-start | bytes 5898244
  66.2 169.1 %collective-permute-start.5 = (bf16[512,1,256]{0,2,1:T(8,128)(2,1)}, bf16[512,1,256]{0,2,1:T(8,128)(2,1)}, u32[]{:S(2)}, u32[]{:S(2)}) collective-permute-start(bf16[512,1,256]{0,2,1:T(8,128)(2,1)} %pad_maximum_fusion), channel_id=1, source_target_pairs={{0,4},{4,8},{8,12},{12,16},{16,20},{20,24},{24,28},{28,32},{32,36}... | collective-permute-start | bytes 786440 | tf_op jit(solution)/shard_map/ppermute | solution.py:17
  68.5 166.8 %collective-permute-start.4 = (bf16[512,1,256]{0,2,1:T(8,128)(2,1)}, bf16[512,1,256]{0,2,1:T(8,128)(2,1)}, u32[]{:S(2)}, u32[]{:S(2)}) collective-permute-start(bf16[512,1,256]{0,2,1:T(8,128)(2,1)} %pad_maximum_fusion), channel_id=1, source_target_pairs={{0,8},{4,12},{8,16},{12,20},{16,24},{20,28},{24,32},{28,36},{32,40... | collective-permute-start | bytes 786440 | tf_op jit(solution)/shard_map/ppermute | solution.py:17
  74.2 164.2 %collective-permute-start.1 = (bf16[512,1,256]{2,0,1:T(8,128)(2,1)}, bf16[512,1,256]{2,0,1:T(8,128)(2,1)}, u32[]{:S(2)}, u32[]{:S(2)}) collective-permute-start(bf16[512,1,256]{2,0,1:T(8,128)(2,1)} %fusion.34), channel_id=1, source_target_pairs={{0,4},{4,8},{8,12},{12,16},{16,20},{20,24},{24,28},{28,32},{32,36}... | collective-permute-start | bytes 786440 | tf_op jit(solution)/shard_map/ppermute | solution.py:17
  78.2 160.2 %collective-permute-start = (bf16[512,1,256]{2,0,1:T(8,128)(2,1)}, bf16[512,1,256]{2,0,1:T(8,128)(2,1)}, u32[]{:S(2)}, u32[]{:S(2)}) collective-permute-start(bf16[512,1,256]{2,0,1:T(8,128)(2,1)} %fusion.34), channel_id=1, source_target_pairs={{0,8},{4,12},{8,16},{12,20},{16,24},{20,28},{24,32},{28,36},{32,40... | collective-permute-start | bytes 786440 | tf_op jit(solution)/shard_map/ppermute | solution.py:17
  226.7 3.8 copy-start.6
  226.7 4.6 %copy-start.8 = (bf16[512,3840]{0,1:T(8,128)(2,1)S(1)}, bf16[512,3840]{0,1:T(8,128)(2,1)}, u32[]{:S(2)}) copy-start(bf16[512,3840]{0,1:T(8,128)(2,1)} %all-gather.4.cloned.1.call-done) | copy-start | bytes 11796484
  233.5 1.4 copy-start.3
  233.8 1.5 copy-start.2
  235.3 3.1 copy-start.10
  238.4 4.5 %copy-start.11 = (f32[1536,512,2]{1,0,2:T(8,128)}, f32[1536,512,2]{1,0,2:T(8,128)S(1)}, u32[]{:S(2)}) copy-start(f32[1536,512,2]{1,0,2:T(8,128)S(1)} %get-tuple-element.21) | copy-start | bytes 18874372
  253.0 149.6 %copy-start.1 = (bf16[3840,256]{1,0:T(8,128)(2,1)S(1)}, bf16[3840,256]{1,0:T(8,128)(2,1)}, u32[]{:S(2)}) copy-start(bf16[3840,256]{1,0:T(8,128)(2,1)} %param.13) | copy-start | bytes 5898244
Sparse Core Ops, SparseCore 0:
  9.8 50.8 all-gather.3
  63.4 84.3 all-gather.5
  150.6 76.0 all-gather.7
  253.1 149.4 reduce-scatter.1
where the time goes:
time: 410 us; the launch traced here: 409 us
  waiting for transfers between devices  295 us (72%)
  matrix products  44.1 us (11%)
  blocking collectives  20.2 us (5%)
  starting transfers between devices  18.7 us (5%)
  between operations  14.1 us (3%)
  other arithmetic  10.1 us (2%)
  local copies, waits for them, and re-layouts  6.79 us (2%)
    reduce_scatter x1, waiting for transfers between devices, local(): lax.psum_scatter(jnp.einsum('acr,ace->are', slot_low_rows, slot_grad_rows...  143 us
    all_gather x1, waiting for transfers between devices, local(): lax.all_gather(adapter_down, 'seq', axis=0, tiled=True)  66.8 us
    all_gather x1, waiting for transfers between devices, local(): lax.all_gather(adapter_up, 'seq', axis=0, tiled=True)  52.3 us
    all_gather x1, waiting for transfers between devices, local(): shard_cols = lax.all_gather(tokens, 'tensor', axis=1, tiled=True)  30.4 us
    psum x1, blocking collectives, local(): slot_low = lax.psum(partial_low, 'tensor').astype(jnp.bfloat16)  20.2 us
    ppermute x6, starting transfers between devices, passed_along(): lax.ppermute(value, axis, [(source, source + steps) for source in range(f...  18.6 us
  transfers between devices with their start and end apart: 10, of which 4 were waited for; matrix products, arithmetic and copies ran while one was open for 11% of the time, Pallas kernels for 0%

commit v1 on v0

--- a/solution.py
+++ b/solution.py
@@ -80,7 +80,9 @@
     kv_heads = kv_width // HD
     head_group = local_heads // kv_heads
     positions = lax.axis_index("seq") * tok_count + jnp.arange(tok_count, dtype=jnp.int32)
-    shard_cols = lax.all_gather(tokens, "tensor", axis=1, tiled=True)
+    shard_cols = jnp.concatenate(
+        lax.all_to_all(jnp.stack([tokens] * lax.axis_size("tensor")), "tensor", 0, 0), axis=1
+    )
     query_lin = jnp.dot(shard_cols, w_query, preferred_element_type=jnp.float32)
     key_lin = jnp.dot(shard_cols, w_key, preferred_element_type=jnp.float32)
     value_lin = jnp.dot(shard_cols, w_value, preferred_element_type=jnp.float32)

time: 410 us -> 368 us (0.90)
  waiting for transfers between devices: 295 us -> 243 us
  starting transfers between devices: 18.7 us -> 25 us
    all_gather x1, waiting for transfers between devices: 66.8 us -> 19.3 us  [local(): lax.all_gather(adapter_down, 'seq', axis=0, tiled=True)]
    all_gather x1 -> x0, waiting for transfers between devices: 30.4 us -> none  [local(): shard_cols = lax.all_gather(tokens, 'tensor', axis=1, tiled=True)]
    all_to_all x0 -> x1, waiting for transfers between devices: none -> 27.3 us  [local(): lax.all_to_all(jnp.stack([tokens] * lax.axis_size('tensor')), 'tensor', 0...]
    all_to_all x0 -> x1, starting transfers between devices: none -> 7.18 us  [local(): lax.all_to_all(jnp.stack([tokens] * lax.axis_size('tensor')), 'tensor', 0...]
  transfers between devices with their start and end apart: 10 -> 10, of which waited for: 4 -> 4; matrix products, arithmetic and copies ran while one was open for 11% -> 14% of each run, Pallas kernels for 0% -> 0%
where the time goes in v1:
time: 368 us
  waiting for transfers between devices  243 us (66%)
  matrix products  47.7 us (13%)
  starting transfers between devices  25 us (7%)
  blocking collectives  20.3 us (6%)
  between operations  14.1 us (4%)
  local copies, waits for them, and re-layouts  9.31 us (3%)
  other arithmetic  8.05 us (2%)
    reduce_scatter x1, waiting for transfers between devices, local(): lax.psum_scatter(jnp.einsum('acr,ace->are', slot_low_rows, slot_grad_rows...  143 us
    all_gather x1, waiting for transfers between devices, local(): lax.all_gather(adapter_up, 'seq', axis=0, tiled=True)  52.1 us
    all_to_all x1, waiting for transfers between devices, local(): lax.all_to_all(jnp.stack([tokens] * lax.axis_size('tensor')), 'tensor', 0...  27.3 us
    psum x1, blocking collectives, local(): slot_low = lax.psum(partial_low, 'tensor').astype(jnp.bfloat16)  20.3 us
    all_gather x1, waiting for transfers between devices, local(): lax.all_gather(adapter_down, 'seq', axis=0, tiled=True)  19.3 us
    ppermute x6, starting transfers between devices, passed_along(): lax.ppermute(value, axis, [(source, source + steps) for source in range(f...  17.7 us
  transfers between devices with their start and end apart: 10, of which 4 were waited for; matrix products, arithmetic and copies ran while one was open for 14% of the time, Pallas kernels for 0%

profile of v1, /device:TPU:2, one launch (start us, length us, event | category | flops | bytes accessed | tf_op | source)
XLA Modules:
  0.0 367.9 jit_solution(12470993814805625501)
XLA Ops:
  7.2 0.0 copy-start
  7.2 0.0 all-gather.3.cloned.1.call-start
  7.2 0.7 all-gather.3.cloned.1.call-update
  7.9 0.0 all-gather.5.cloned.1.call-start
  8.0 0.7 all-gather.5.cloned.1.call-update
  8.7 3.4 stack.2
  12.1 7.2 %all-to-all-start = ((bf16[4,512,960]{1,2,0:T(8,128)(2,1)}), bf16[4,512,960]{1,2,0:T(8,128)(2,1)}, u32[]{:S(2)}, u32[]{:S(2)}) async-start(bf16[4,512,960]{1,2,0:T(8,128)(2,1)} %stack.2), calls=%async_computation | async-start | bytes 7864320 | tf_op jit(solution)/shard_map/all_to_all | solution.py:84
  19.2 0.0 reduce-scatter.2.cloned.1.call-start
  19.2 0.0 copy-done.6
  19.2 1.3 collective-permute-start.3
  20.5 2.7 collective-permute-start.2
  23.3 1.2 reduce-window.6
  24.5 0.2 slice_reduce_fusion
  24.9 0.1 fusion.59
  25.0 1.0 multiply_cosine_fusion
  26.0 2.5 fusion.24
  28.5 3.9 %copy.41 = bf16[1024,960]{1,0:T(8,128)(2,1)} copy(bf16[1024,960]{0,1:T(8,128)(2,1)} %fusion.24) | data formatting | bytes 3932160 | tf_op jit(solution)/shard_map/convert_element_type | solution.py:97
  32.4 0.0 collective-permute-done.3
  32.4 0.0 collective-permute-done.2
  32.4 2.5 fusion.16
  35.0 27.3 %all-to-all-done = bf16[4,512,960]{1,2,0:T(8,128)(2,1)} async-done(((bf16[4,512,960]{1,2,0:T(8,128)(2,1)}), bf16[4,512,960]{1,2,0:T(8,128)(2,1)}, u32[]{:S(2)}, u32[]{:S(2)}) %all-to-all-start) | async-done | bytes 3932192 | tf_op jit(solution)/shard_map/all_to_all | solution.py:84
  62.2 4.0 %multiply_reduce_fusion.2 = (f32[512]{0:T(512)S(1)}, f32[512,256]{0,1:T(8,128)S(1)}) fusion(bf16[512,3840]{0,1:T(8,128)(2,1)} %bitcast.1, bf16[3840,256]{1,0:T(8,128)(2,1)S(1)} %copy-done), kind=kOutput, calls=%fused_computation.63 | convolution fusion | flops 1006894592 | bytes 6424576 | tf_op jit(solution)/shard_map/dot_general | solution.py:87
  66.3 0.1 multiply_bitcast_fusion
  66.4 1.2 fusion.55
  67.6 0.7 pad_maximum_fusion
  68.3 2.0 collective-permute-start.5
  70.3 4.4 %collective-permute-start.4 = (bf16[512,1,256]{0,2,1:T(8,128)(2,1)}, bf16[512,1,256]{0,2,1:T(8,128)(2,1)}, u32[]{:S(2)}, u32[]{:S(2)}) collective-permute-start(bf16[512,1,256]{0,2,1:T(8,128)(2,1)} %pad_maximum_fusion), channel_id=1, source_target_pairs={{0,8},{4,12},{8,16},{12,20},{16,24},{20,28},{24,32},{28,36},{32,40... | collective-permute-start | bytes 786440 | tf_op jit(solution)/shard_map/ppermute | solution.py:17
  74.6 4.1 %fusion.34 = bf16[512,1,256]{2,0,1:T(8,128)(2,1)} fusion(bf16[512,3840]{0,1:T(8,128)(2,1)} %bitcast.1, bf16[3840,256]{1,0:T(8,128)(2,1)S(1)} %copy-done.9), kind=kOutput, calls=%fused_computation.37 | convolution fusion | flops 1006764032 | bytes 6160384 | tf_op jit(solution)/shard_map/dot_general | solution.py:88
  78.7 4.1 %collective-permute-start.1 = (bf16[512,1,256]{2,0,1:T(8,128)(2,1)}, bf16[512,1,256]{2,0,1:T(8,128)(2,1)}, u32[]{:S(2)}, u32[]{:S(2)}) collective-permute-start(bf16[512,1,256]{2,0,1:T(8,128)(2,1)} %fusion.34), channel_id=1, source_target_pairs={{0,4},{4,8},{8,12},{12,16},{16,20},{20,24},{24,28},{28,32},{32,36}... | collective-permute-start | bytes 786440 | tf_op jit(solution)/shard_map/ppermute | solution.py:17
  82.8 3.3 collective-permute-start
  86.1 19.3 %all-gather.3.cloned.1.call-done = bf16[64,64,960]{2,1,0:T(8,128)(2,1)} async-done(((bf16[1,64,960]{2,1,0:T(8,128)(2,1)}), bf16[64,64,960]{2,1,0:T(8,128)(2,1)}) %all-gather.3.cloned.1.call-update) | async-done | bytes 7864336 | tf_op jit(solution)/shard_map/all_gather | solution.py:99
  105.5 6.3 %fusion.73 = f32[64,16,64]{2,1,0:T(8,128)S(1)} fusion(bf16[64,16,960]{2,1,0:T(8,128)(2,1)} %bitcast.131, bf16[64,64,960]{2,1,0:T(8,128)(2,1)} %all-gather.3.cloned.1.call-done), kind=kOutput, calls=%fused_computation.106 | convolution fusion | flops 125829120 | bytes 10092544 | tf_op jit(solution)/shard_map/acd,ard->acr/dot_general | solution.py:103
  111.7 20.3 %all-reduce.3 = bf16[64,16,64]{2,1,0:T(8,128)(2,1)S(1)} all-reduce(f32[64,16,64]{2,1,0:T(8,128)S(1)} %fusion.73), channel_id=1, replica_groups=mesh['seq'=64,'tensor'=4] {'tensor'}, use_global_device_ids=true, to_apply=%region_4.5 | all-reduce | flops 65536 | bytes 393216 | tf_op jit(solution)/shard_map/psum | solution.py:106
  132.1 52.1 %all-gather.5.cloned.1.call-done = bf16[64,64,512]{2,1,0:T(8,128)(2,1)} async-done(((bf16[1,64,512]{2,1,0:T(8,128)(2,1)}), bf16[64,64,512]{2,1,0:T(8,128)(2,1)}) %all-gather.5.cloned.1.call-update) | async-done | bytes 4194320 | tf_op jit(solution)/shard_map/all_gather | solution.py:100
  184.1 3.0 convolution_convert_fusion
  187.1 0.8 fusion.30
  187.9 4.4 %multiply_reduce_fusion.1 = (f32[512,2]{0,1:T(2,128)S(1)}, f32[512,512]{0,1:T(8,128)S(1)}) fusion(f32[512,512]{0,1:T(8,128)S(1)} %fusion.30, bf16[512,3840]{0,1:T(8,128)(2,1)} %bitcast.1, bf16[3840,512]{1,0:T(8,128)(2,1)S(1)} %copy-done.8), kind=kOutput, calls=%fused_computation.44 | convolution fusion | flops 2014051328 | bytes 9965568 | tf_op jit(solution)/shard_map/dot_general | solution.py:86
  192.3 0.0 copy-start.5
  192.3 0.3 copy.42
  192.7 0.9 fusion.35
  193.6 0.2 copy.46
  193.8 0.2 multiply_multiply_fusion
  194.0 0.1 subtract_convert_fusion
  194.1 0.0 collective-permute-done.5
  194.1 0.0 collective-permute-done.4
  194.1 0.0 copy-done.3
  194.2 0.0 copy-start.10
  194.2 3.1 fusion.5
  197.3 0.0 copy-start.11
  197.3 0.0 collective-permute-done.1
  197.3 0.0 collective-permute-done
  197.3 4.4 %fusion = (f32[2,512]{1,0:T(2,128)S(1)}, f32[1536,512,2]{1,0,2:T(8,128)S(1)}) fusion(f32[2,512]{1,0:T(2,128)S(1)} %get-tuple-element.20, f32[1536,512,2]{1,0,2:T(8,128)S(1)} %get-tuple-element.21, pred[512,1536]{0,1:T(8,128)(4,1)S(1)} %copy-done.3, bf16[64,2,8,256]{3,2,1,0:T(8,128)(2,1)S(1)} %bitcast.142, bf16[512,1,256]{2,0,1:T(8,128)(2,1)} %fusion.34, ...), kind=kOutput, calls=%fused_computation.3 | convolution fusion | flops 815528960 | bytes 14688256 | tf_op jit(solution)/shard_map/tngd,knd->ngtk/dot_general | solution.py:55
  201.7 3.8 %fusion.26 = f32[512,2,256]{2,0,1:T(8,128)S(1)} fusion(f32[1536,512,2]{1,0,2:T(8,128)S(1)} %get-tuple-element.23, f32[2,512]{1,0:T(2,128)S(1)} %get-tuple-element.22, f32[2,512]{1,0:T(2,128)S(1)} %get-tuple-element.20, f32[1536,512,2]{1,0,2:T(8,128)S(1)} %get-tuple-element.21, pred[512,1536]{0,1:T(8,128)(4,1)S(1)} %copy-done.3, ...), kind=kOutput, calls=%fused_computation.31 | convolution fusion | flops 819462144 | bytes 15212544 | tf_op jit(solution)/shard_map/ngtk,knd->tngd/dot_general | solution.py:58
  205.5 0.2 multiply_add_fusion.1
  205.7 0.3 multiply_reduce_fusion
  205.9 0.4 fusion.37
  206.3 0.2 copy.52
  206.5 0.7 fusion.25
  207.3 4.5 %fusion.74 = f32[64,64,512]{2,1,0:T(8,128)} fusion(bf16[64,16,64]{2,1,0:T(8,128)(2,1)S(1)} %bitcast.133, bf16[64,16,512]{2,1,0:T(8,128)(2,1)S(1)} %bitcast.132), kind=kOutput, calls=%fused_computation.107 | convolution fusion | flops 67108864 | bytes 9568256 | tf_op jit(solution)/shard_map/acr,ace->are/dot_general | solution.py:169
  211.8 0.0 reduce-scatter.2.cloned.1.call-update
  211.8 0.0 copy-start.1
  211.8 5.2 %fusion.31 = bf16[256,2,512]{2,0,1:T(8,128)(2,1)S(1)} fusion(f32[2,512]{1,0:T(2,128)S(1)} %get-tuple-element.20, f32[1536,512,2]{1,0,2:T(8,128)} %copy-done.11, pred[512,1536]{0,1:T(8,128)(4,1)S(1)} %copy-done.3, bf16[512,1,256]{2,0,1:T(8,128)(2,1)} %fusion.34, bf16[512,1,256]{2,0,1:T(8,128)(2,1)} %collective-permute-done.1, ...), kind=kOutput, calls=%fused_computation.35 | convolution fusion | flops 814219264 | bytes 8392704 | tf_op jit(solution)/shard_map/ngtk,knd->tngd/dot_general | solution.py:54
  217.0 1.0 copy.53
  218.0 143.3 %reduce-scatter.2.cloned.1.call-done = f32[1,64,512]{2,1,0:T(8,128)} async-done(((f32[64,64,512]{2,1,0:T(8,128)}), f32[1,64,512]{2,1,0:T(8,128)}) %reduce-scatter.2.cloned.1.call-update) | async-done | bytes 131088 | tf_op jit(solution)/shard_map/reduce_scatter | solution.py:168
  (31 shorter events, 0.2 us)
Async XLA Ops:
  7.2 55.1 %copy-start = (bf16[3840,256]{1,0:T(8,128)(2,1)S(1)}, bf16[3840,256]{1,0:T(8,128)(2,1)}, u32[]{:S(2)}) copy-start(bf16[3840,256]{1,0:T(8,128)(2,1)} %param.13) | copy-start | bytes 5898244
  7.2 98.3 %all-gather.3.cloned.1.call-start = ((), (), s32[]{:S(2)}) async-start(), calls=%async_computation.2 | async-start | bytes 8519680 | tf_op jit(solution)/shard_map/all_gather | solution.py:99
  7.9 176.2 %all-gather.5.cloned.1.call-start = ((), (), s32[]{:S(2)}) async-start(), calls=%async_computation.3 | async-start | bytes 4259840 | tf_op jit(solution)/shard_map/all_gather | solution.py:100
  12.1 7.2 %copy-start.6 = (s32[512]{0:T(512)S(1)}, s32[512]{0:T(512)}, u32[]{:S(2)}) copy-start(s32[512]{0:T(512)} %param.20) | copy-start | bytes 6148
  12.1 11.2 %copy-start.4 = (s32[512,1]{0,1:T(1,128)S(1)}, s32[512,1]{0,1:T(1,128)}, u32[]{:S(2)}) copy-start(s32[512,1]{0,1:T(1,128)} %param.19) | copy-start | bytes 6148
  12.1 13.9 %copy-start.2 = (bf16[512,960]{0,1:T(8,128)(2,1)S(1)}, bf16[512,960]{0,1:T(8,128)(2,1)}, u32[]{:S(2)}) copy-start(bf16[512,960]{0,1:T(8,128)(2,1)} %param.11) | copy-start | bytes 2949124
  12.1 50.2 %all-to-all-start = ((bf16[4,512,960]{1,2,0:T(8,128)(2,1)}), bf16[4,512,960]{1,2,0:T(8,128)(2,1)}, u32[]{:S(2)}, u32[]{:S(2)}) async-start(bf16[4,512,960]{1,2,0:T(8,128)(2,1)} %stack.2), calls=%async_computation | async-start | bytes 7864320 | tf_op jit(solution)/shard_map/all_to_all | solution.py:84
  19.2 342.1 %reduce-scatter.2.cloned.1.call-start = ((), (), s32[]{:S(2)}) async-start(), calls=%async_computation.4 | async-start | bytes 8519680 | tf_op jit(solution)/shard_map/reduce_scatter | solution.py:168
  19.2 13.2 %collective-permute-start.3 = (s32[512]{0:T(512)S(1)}, s32[512]{0:T(512)S(1)}, u32[]{:S(2)}, u32[]{:S(2)}) collective-permute-start(s32[512]{0:T(512)S(1)} %copy-done.6), channel_id=1, source_target_pairs={{0,4},{4,8},{8,12},{12,16},{16,20},{20,24},{24,28},{28,32},{32,36}... | collective-permute-start | bytes 6152 | tf_op jit(solution)/shard_map/ppermute | solution.py:17
  20.5 11.9 %collective-permute-start.2 = (s32[512]{0:T(512)S(1)}, s32[512]{0:T(512)S(1)}, u32[]{:S(2)}, u32[]{:S(2)}) collective-permute-start(s32[512]{0:T(512)S(1)} %copy-done.6), channel_id=1, source_target_pairs={{0,8},{4,12},{8,16},{12,20},{16,24},{20,28},{24,32},{28,36},{32,40... | collective-permute-start | bytes 6152 | tf_op jit(solution)/shard_map/ppermute | solution.py:17
  62.2 4.0 %copy-start.7 = (f32[256]{0:T(256)S(1)}, f32[256]{0:T(256)}, u32[]{:S(2)}) copy-start(f32[256]{0:T(256)} %param.16) | copy-start | bytes 3076
  62.2 12.4 %copy-start.9 = (bf16[3840,256]{1,0:T(8,128)(2,1)S(1)}, bf16[3840,256]{1,0:T(8,128)(2,1)}, u32[]{:S(2)}) copy-start(bf16[3840,256]{1,0:T(8,128)(2,1)} %param.14) | copy-start | bytes 5898244
  68.3 125.8 %collective-permute-start.5 = (bf16[512,1,256]{0,2,1:T(8,128)(2,1)}, bf16[512,1,256]{0,2,1:T(8,128)(2,1)}, u32[]{:S(2)}, u32[]{:S(2)}) collective-permute-start(bf16[512,1,256]{0,2,1:T(8,128)(2,1)} %pad_maximum_fusion), channel_id=1, source_target_pairs={{0,4},{4,8},{8,12},{12,16},{16,20},{20,24},{24,28},{28,32},{32,36}... | collective-permute-start | bytes 786440 | tf_op jit(solution)/shard_map/ppermute | solution.py:17
  70.3 123.9 %collective-permute-start.4 = (bf16[512,1,256]{0,2,1:T(8,128)(2,1)}, bf16[512,1,256]{0,2,1:T(8,128)(2,1)}, u32[]{:S(2)}, u32[]{:S(2)}) collective-permute-start(bf16[512,1,256]{0,2,1:T(8,128)(2,1)} %pad_maximum_fusion), channel_id=1, source_target_pairs={{0,8},{4,12},{8,16},{12,20},{16,24},{20,28},{24,32},{28,36},{32,40... | collective-permute-start | bytes 786440 | tf_op jit(solution)/shard_map/ppermute | solution.py:17
  78.7 118.5 %collective-permute-start.1 = (bf16[512,1,256]{2,0,1:T(8,128)(2,1)}, bf16[512,1,256]{2,0,1:T(8,128)(2,1)}, u32[]{:S(2)}, u32[]{:S(2)}) collective-permute-start(bf16[512,1,256]{2,0,1:T(8,128)(2,1)} %fusion.34), channel_id=1, source_target_pairs={{0,4},{4,8},{8,12},{12,16},{16,20},{20,24},{24,28},{28,32},{32,36}... | collective-permute-start | bytes 786440 | tf_op jit(solution)/shard_map/ppermute | solution.py:17
  82.8 114.4 %collective-permute-start = (bf16[512,1,256]{2,0,1:T(8,128)(2,1)}, bf16[512,1,256]{2,0,1:T(8,128)(2,1)}, u32[]{:S(2)}, u32[]{:S(2)}) collective-permute-start(bf16[512,1,256]{2,0,1:T(8,128)(2,1)} %fusion.34), channel_id=1, source_target_pairs={{0,8},{4,12},{8,16},{12,20},{16,24},{20,28},{24,32},{28,36},{32,40... | collective-permute-start | bytes 786440 | tf_op jit(solution)/shard_map/ppermute | solution.py:17
  184.1 3.8 %copy-start.8 = (bf16[3840,512]{1,0:T(8,128)(2,1)S(1)}, bf16[3840,512]{1,0:T(8,128)(2,1)}, u32[]{:S(2)}) copy-start(bf16[3840,512]{1,0:T(8,128)(2,1)} %param.12) | copy-start | bytes 11796484
  192.3 1.4 copy-start.5
  192.7 1.5 copy-start.3
  194.2 3.1 copy-start.10
  197.3 4.5 %copy-start.11 = (f32[1536,512,2]{1,0,2:T(8,128)}, f32[1536,512,2]{1,0,2:T(8,128)S(1)}, u32[]{:S(2)}) copy-start(f32[1536,512,2]{1,0,2:T(8,128)S(1)} %get-tuple-element.21) | copy-start | bytes 18874372
  211.8 149.6 %copy-start.1 = (bf16[3840,256]{1,0:T(8,128)(2,1)S(1)}, bf16[3840,256]{1,0:T(8,128)(2,1)}, u32[]{:S(2)}) copy-start(bf16[3840,256]{1,0:T(8,128)(2,1)} %param.13) | copy-start | bytes 5898244
Sparse Core Ops, SparseCore 0:
  10.8 94.6 all-gather.2
  108.2 75.8 all-gather.4
  211.9 149.3 reduce-scatter.1
